TPU v7x, 256 devices: a whole 4x4x8 slice. The times are simulated.
256 devices in a mesh: seq: 64 (over z, y, core), ch: 4 (over x).
Axes of the slice: x: 4, y: 4, z: 8, core: 2. Of those that a mesh axis runs over, the one named last changes fastest.
Arguments:
- query_proj: bfloat16 [8192, 2048], P('seq', 'ch'), may hold values from -6 to 6
- key_proj: bfloat16 [8192, 2048], P('seq', 'ch'), may hold values from -6 to 6
- value_proj: bfloat16 [8192, 2048], P('seq', 'ch'), may hold values from -6 to 6
- short_filter: float32 [3, 3, 2048], P(None, None, 'ch'), may hold values from -3.5 to 3.5
- long_filter: float32 [8192, 2048], P('seq', 'ch'), may hold values from -0.0625 to 0.0625
- skip_gain: float32 [2048], P('ch'), may hold values from 0.5 to 1.5
- out_weight: bfloat16 [2048, 4096], P('ch'), may hold values from -0.125 to 0.125
- cotangent: bfloat16 [8192, 4096], P('seq', 'ch'), may hold values from -16 to 16
Outputs:
- layer_out: bfloat16 [8192, 4096], P('seq', 'ch')
- grad_query: float32 [8192, 2048], P('seq', 'ch')
- grad_key: float32 [8192, 2048], P('seq', 'ch')
- grad_value: float32 [8192, 2048], P('seq', 'ch')
- grad_short: float32 [3, 3, 2048], P(None, None, 'ch')
- grad_filter: float32 [8192, 2048], P('seq', 'ch')
- grad_skip: float32 [2048], P('ch')
- grad_w_out_t: float32 [4096, 2048], P('seq', 'ch')
All inputs are finite; a program needn't handle non-finite values.
Results may differ from a plain program's by a relative error of at most 0.011.
Values may be sent and summed in bfloat16 or wider, within the bound.
A program may use at most 128 MiB of HBM per device.

v0:
```python
import functools
import math

import jax
import jax.numpy as jnp
from jax import lax
from jax.experimental import pallas as pl
from jax.experimental.pallas import tpu as pltpu
from jax.sharding import PartitionSpec as P

exact_mode = lax.Precision.HIGHEST
SEQ = ("seq_hi", "seq_lo")


def from_behind(shard, axis, by):
    size = lax.axis_size(axis)
    pairs = [(i, i + by) for i in range(size) if 0 <= i + by < size]
    return lax.ppermute(shard, axis, pairs)


def as_sent(shard):

    def short(part):
        return part.astype(jnp.bfloat16) if part.dtype == jnp.float32 else part

    return jax.tree.map(short, shard)


def group_sum_kernel(axis, blocks_ref, out_ref, slots, local_sem, send_sems, recv_sems):
    count = lax.axis_size(axis)
    me = lax.axis_index(axis)
    place = {"seq_hi": lax.axis_index("seq_hi"), "seq_lo": lax.axis_index("seq_lo")}

    def member(index):
        where = dict(place, **{axis: index})
        return (where["seq_hi"], where["seq_lo"], lax.axis_index("ch"))

    barrier = pltpu.get_barrier_semaphore()
    for step in range(1, count):
        pl.semaphore_signal(
            barrier,
            1,
            device_id=member(lax.rem(me + step, count)),
            device_id_type=pl.DeviceIdType.MESH,
        )
    pl.semaphore_wait(barrier, count - 1)
    own = pltpu.make_async_copy(blocks_ref.at[me], slots.at[me], local_sem)
    own.start()
    outgoing = []
    for step in range(1, count):
        peer = lax.rem(me + step, count)
        copy = pltpu.make_async_remote_copy(
            src_ref=blocks_ref.at[peer],
            dst_ref=slots.at[me],
            send_sem=send_sems.at[step],
            recv_sem=recv_sems.at[me],
            device_id=member(peer),
            device_id_type=pl.DeviceIdType.MESH,
        )
        copy.start()
        outgoing.append(copy)
    own.wait()
    for step in range(1, count):
        source = lax.rem(me + count - step, count)
        outgoing[step - 1].wait_send()
        pltpu.make_async_remote_copy(
            src_ref=blocks_ref.at[source],
            dst_ref=slots.at[source],
            send_sem=send_sems.at[step],
            recv_sem=recv_sems.at[source],
            device_id=member(source),
            device_id_type=pl.DeviceIdType.MESH,
        ).wait_recv()
    total = slots[0]
    for slot in range(1, count):
        total = total + slots[slot]
    out_ref[...] = total


def sum_over_group(blocks, axis, kernel_id):
    count = blocks.shape[0]
    return pl.pallas_call(
        functools.partial(group_sum_kernel, axis),
        out_shape=jax.ShapeDtypeStruct(blocks.shape[1:], blocks.dtype),
        in_specs=[pl.BlockSpec(memory_space=pltpu.VMEM)],
        out_specs=pl.BlockSpec(memory_space=pltpu.VMEM),
        scratch_shapes=[
            pltpu.VMEM(blocks.shape, blocks.dtype),
            pltpu.SemaphoreType.DMA(()),
            pltpu.SemaphoreType.DMA((count,)),
            pltpu.SemaphoreType.DMA((count,)),
        ],
        compiler_params=pltpu.CompilerParams(collective_id=kernel_id, has_side_effects=True),
    )(blocks)


def split_lanes(merged, lanes):
    return tuple(
        merged[..., start : start + lanes] for start in range(0, merged.shape[-1], lanes)
    )


def tables(rows_out, cols_in, period):
    row_index = lax.broadcasted_iota(jnp.int32, (rows_out, cols_in), 0)
    col_index = lax.broadcasted_iota(jnp.int32, (rows_out, cols_in), 1)
    phase_angle = (row_index * col_index % period).astype(jnp.float32) * (2.0 * math.pi / period)
    return (jnp.cos(phase_angle), jnp.sin(phase_angle))


def odd_tables(rows_out, cols_in, period, odd_axis):
    row_index = lax.broadcasted_iota(jnp.int32, (rows_out, cols_in), 0)
    col_index = lax.broadcasted_iota(jnp.int32, (rows_out, cols_in), 1)
    if odd_axis == 0:
        row_index = 2 * row_index + 1
    else:
        col_index = 2 * col_index + 1
    phase_angle = (row_index * col_index % (2 * period)).astype(jnp.float32) * (math.pi / period)
    return (jnp.cos(phase_angle), jnp.sin(phase_angle))


def along_rows(factor, values):
    return jnp.tensordot(factor, values, axes=1, precision=exact_mode)


def rows_spectrum(signal, basis_pair):
    return (along_rows(basis_pair[0], signal), -along_rows(basis_pair[1], signal))


def rows_inverse(complex_pair, basis_pair):
    total = along_rows(basis_pair[0], complex_pair[0]) - along_rows(basis_pair[1], complex_pair[1])
    return total / basis_pair[0].shape[1]


def block_forward(complex_pair, basis_pair):
    cosine_part, sine_part = basis_pair
    real_part = along_rows(cosine_part, complex_pair[0]) + along_rows(sine_part, complex_pair[1])
    imag_part = along_rows(cosine_part, complex_pair[1]) - along_rows(sine_part, complex_pair[0])
    return (real_part, imag_part)


def block_inverse(complex_pair, basis_pair):
    cosine_part, sine_part = basis_pair
    norming = 1.0 / cosine_part.shape[1]
    real_part = along_rows(cosine_part, complex_pair[0]) - along_rows(sine_part, complex_pair[1])
    imag_part = along_rows(cosine_part, complex_pair[1]) + along_rows(sine_part, complex_pair[0])
    return (real_part * norming, imag_part * norming)


def complex_product(first_pair, second_pair):
    return (
        first_pair[0] * second_pair[0] - first_pair[1] * second_pair[1],
        first_pair[0] * second_pair[1] + first_pair[1] * second_pair[0],
    )


def conj_product(first_pair, second_pair):
    return (
        first_pair[0] * second_pair[0] + first_pair[1] * second_pair[1],
        first_pair[0] * second_pair[1] - first_pair[1] * second_pair[0],
    )


def on_device(
    query_proj, key_proj, value_proj, short_filter, long_filter, skip_gain, out_weight, cotangent
):
    block_rows = query_proj.shape[0]
    tap_count = short_filter.shape[1]
    block_count = lax.axis_size(SEQ)
    streams = jnp.stack([query_proj, key_proj, value_proj])
    earlier = from_behind(streams[:, block_rows - (tap_count - 1) :], SEQ, 1)
    extended = jnp.concatenate([earlier, streams], axis=1).astype(jnp.float32)
    shifted = [
        extended[:, tap_count - 1 - offset : tap_count - 1 - offset + block_rows]
        for offset in range(tap_count)
    ]
    filtered = sum(
        (short_filter[:, offset][:, None, :] * shifted[offset] for offset in range(tap_count))
    )
    query_short, key_short, value_short = (filtered[0], filtered[1], filtered[2])
    product = key_short * value_short
    forward_basis = odd_tables(block_rows, block_rows, 2 * block_rows, 0)
    spread_basis = odd_tables(block_rows, 2 * block_rows, 2 * block_rows, 0)
    fold_basis = odd_tables(2 * block_rows, block_rows, 2 * block_rows, 1)
    half_basis = odd_tables(block_rows, block_rows, 2 * block_rows, 1)
    block_basis = tables(2 * block_count, block_count, 2 * block_count)
    return_basis = tables(block_count, 2 * block_count, 2 * block_count)
    input_pair = rows_spectrum(product, forward_basis)
    filter_pair = rows_spectrum(long_filter, forward_basis)
    lanes = product.shape[1]
    moved_data = split_lanes(
        lax.all_to_all(
            jnp.concatenate([input_pair[0], input_pair[1], filter_pair[0], filter_pair[1]], axis=1)[
                None
            ],
            SEQ,
            split_axis=1,
            concat_axis=0,
            tiled=True,
        ),
        lanes,
    )
    input_spectrum = block_forward((moved_data[0], moved_data[1]), block_basis)
    filter_spectrum = block_forward((moved_data[2], moved_data[3]), block_basis)
    inverse_pair = block_inverse(complex_product(filter_spectrum, input_spectrum), return_basis)
    returned = split_lanes(
        lax.all_to_all(
            jnp.concatenate(inverse_pair, axis=-1), SEQ, split_axis=0, concat_axis=1, tiled=True
        ),
        lanes,
    )
    folded = rows_inverse((returned[0][0], returned[1][0]), fold_basis)
    carried = from_behind(folded[block_rows:], SEQ, 1)
    convolved = folded[:block_rows] + carried
    mixed_seq = convolved + skip_gain * product
    gated_values = (query_short * mixed_seq).astype(jnp.bfloat16)
    full_cotangent = lax.all_gather(cotangent, "ch", axis=1, tiled=True)
    full_cotangent, gated_values = lax.optimization_barrier((full_cotangent, gated_values))
    partial_value = jnp.dot(gated_values, out_weight, preferred_element_type=jnp.float32)
    layer_out = lax.psum_scatter(partial_value, "ch", scatter_dimension=1, tiled=True).astype(
        jnp.bfloat16
    )
    grad_gated = lax.dot_general(
        full_cotangent, out_weight, (((1,), (1,)), ((), ())), preferred_element_type=jnp.float32
    )
    outer = lax.axis_size("seq_hi")
    inner = lax.axis_size("seq_lo")
    feature_rows = full_cotangent.shape[1] // outer // inner
    local_rows = lax.all_gather(gated_values, "seq_hi", axis=0, tiled=True)
    local_features = lax.all_to_all(
        full_cotangent.reshape(block_rows, outer, inner, feature_rows),
        "seq_hi",
        split_axis=1,
        concat_axis=0,
        tiled=True,
    ).reshape(block_rows * outer, -1)
    weight_terms = lax.dot_general(
        local_features,
        local_rows,
        (((0,), (0,)), ((), ())),
        preferred_element_type=jnp.float32,
    )
    grad_mixed = grad_gated * query_short
    grad_query_short = grad_gated * mixed_seq
    following = from_behind(grad_mixed.astype(jnp.bfloat16), SEQ, -1).astype(grad_mixed.dtype)
    spread = jnp.concatenate([grad_mixed, following], axis=0)
    grad_pair = rows_spectrum(spread, spread_basis)
    moved_grad = split_lanes(
        lax.all_to_all(
            jnp.concatenate(grad_pair, axis=1)[None].astype(jnp.bfloat16),
            SEQ,
            split_axis=1,
            concat_axis=0,
            tiled=True,
        ).astype(jnp.float32),
        lanes,
    )
    grad_spectrum = block_forward(moved_grad, block_basis)
    input_back = block_inverse(conj_product(filter_spectrum, grad_spectrum), return_basis)
    filter_back = block_inverse(conj_product(input_spectrum, grad_spectrum), return_basis)
    returned_grad = split_lanes(
        lax.all_to_all(
            as_sent(jnp.concatenate(input_back + filter_back, axis=-1)),
            SEQ,
            split_axis=0,
            concat_axis=1,
            tiled=True,
        ),
        lanes,
    )
    weight_terms, layer_out, returned_grad = lax.optimization_barrier(
        (weight_terms, layer_out, returned_grad)
    )
    conv_grad = rows_inverse((returned_grad[0][0], returned_grad[1][0]), half_basis)
    grad_filter = rows_inverse((returned_grad[2][0], returned_grad[3][0]), half_basis)
    grad_product = conv_grad + skip_gain * grad_mixed
    grad_streams = jnp.stack(
        [grad_query_short, grad_product * value_short, grad_product * key_short]
    )
    later_rows = from_behind(grad_streams[:, : tap_count - 1], SEQ, -1)
    padded_grad = jnp.concatenate([grad_streams, later_rows], axis=1)
    grad_inputs = sum(
        (
            short_filter[:, offset][:, None, :] * padded_grad[:, offset : offset + block_rows]
            for offset in range(tap_count)
        )
    )
    short_terms = jnp.stack(
        [jnp.sum(grad_streams * shifted[offset], axis=1) for offset in range(tap_count)], axis=1
    )
    skip_terms = jnp.sum(grad_mixed * product, axis=0)
    channel_count = skip_terms.shape[0]
    sum_rows = short_terms.shape[0] * short_terms.shape[1] + 1
    padded_rows = -(-sum_rows // 8) * 8
    small_terms = jnp.concatenate(
        [
            short_terms.reshape(sum_rows - 1, channel_count),
            skip_terms[None],
            jnp.zeros((padded_rows - sum_rows, channel_count), jnp.float32),
        ]
    )
    outer_sum = sum_over_group(
        jnp.broadcast_to(small_terms, (outer,) + small_terms.shape), "seq_hi", 0
    )
    weight_blocks = weight_terms.reshape(inner, -1, channel_count)
    block_height = weight_blocks.shape[1]
    reduced = sum_over_group(
        jnp.concatenate(
            [weight_blocks, jnp.broadcast_to(outer_sum, (inner,) + outer_sum.shape)], axis=1
        ),
        "seq_lo",
        1,
    )
    grad_w_out_t = reduced[:block_height]
    summed = reduced[block_height:]
    grad_short = summed[: sum_rows - 1].reshape(short_terms.shape)
    grad_skip = summed[sum_rows - 1]
    return (
        layer_out,
        grad_inputs[0],
        grad_inputs[1],
        grad_inputs[2],
        grad_short,
        grad_filter,
        grad_skip,
        grad_w_out_t,
    )


def solution(mesh):
    in_specs = (
        P(SEQ, "ch"),
        P(SEQ, "ch"),
        P(SEQ, "ch"),
        P(None, None, "ch"),
        P(SEQ, "ch"),
        P("ch"),
        P("ch", None),
        P(SEQ, "ch"),
    )
    out_specs = (
        P(SEQ, "ch"),
        P(SEQ, "ch"),
        P(SEQ, "ch"),
        P(SEQ, "ch"),
        P(None, None, "ch"),
        P(SEQ, "ch"),
        P("ch"),
        P(SEQ, "ch"),
    )
    inner = 8
    seq_mesh = jax.sharding.Mesh(
        mesh.devices.reshape(mesh.shape["seq"] // inner, inner, mesh.shape["ch"]),
        ("seq_hi", "seq_lo", "ch"),
    )
    return jax.shard_map(
        on_device, mesh=seq_mesh, in_specs=in_specs, out_specs=out_specs, check_vma=False
    )
```

profile of v0, /device:TPU:1, one launch (start us, length us, event | category | flops | bytes accessed | tf_op | source)
XLA Modules:
  0.0 295.6 jit_solution(16242245169059082142)
XLA Ops:
  8.0 4.6 %collective-permute-start = (bf16[3,2,512]{2,1,0:T(2,128)(2,1)S(1)}, bf16[3,2,512]{2,1,0:T(2,128)(2,1)S(1)}, u32[]{:S(2)}, u32[]{:S(2)}) collective-permute-start(bf16[3,2,512]{2,1,0:T(2,128)(2,1)S(1)} %pad_maximum_fusion.10), channel_id=1, source_target_pairs={{0,4},{4,8},{8,12},{12,16},{16,20},{20,24},{24,28},{28,32},{32,36}... | collective-permute-start | bytes 18440 | tf_op jit(solution)/shard_map/ppermute | solution.py:18
  18.9 40.2 %all_to_all.63 = f32[1,128,2048]{2,0,1:T(1,128)S(1)} all-to-all(f32[1,128,2048]{2,0,1:T(1,128)S(1)} %copy.39), channel_id=1, replica_groups=mesh['seq_hi'=8,'seq_lo'=8,'ch'=4] {'seq_hi','seq_lo'}, dimensions={1} | all-to-all | bytes 2097152 | tf_op jit(solution)/shard_map/all_to_all | solution.py:191
  59.0 3.7 %reduce = f32[128,2048]{1,0:T(8,128)} reduce(f32[1,128,2048]{2,0,1:T(1,128)S(1)} %all_to_all.63, f32[]{:T(128)} %constant.83), dimensions={0}, to_apply=%all_to_all.22.reduce_sub_computation | reduce | bytes 2097156 | tf_op jit(solution)/shard_map/all_to_all | solution.py:191
  75.4 6.7 %all-to-all-start.1 = ((f32[64,2,1024]{2,1,0:T(2,128)}), f32[64,2,1024]{2,1,0:T(2,128)}, u32[]{:S(2)}, u32[]{:S(2)}) async-start(f32[64,2,1024]{2,1,0:T(2,128)} %copy.44), calls=%async_computation.1 | async-start | bytes 1048576 | tf_op jit(solution)/shard_map/all_to_all | solution.py:206
  84.0 15.7 %all-to-all-done.1 = f32[64,2,1024]{2,1,0:T(2,128)} async-done(((f32[64,2,1024]{2,1,0:T(2,128)}), f32[64,2,1024]{2,1,0:T(2,128)}, u32[]{:S(2)}, u32[]{:S(2)}) %all-to-all-start.1) | async-done | bytes 524320 | tf_op jit(solution)/shard_map/all_to_all | solution.py:206
  99.8 2.2 all_to_all.50
  103.9 2.0 fusion
  106.0 3.4 %collective-permute-start.1 = (f32[128,512]{1,0:T(8,128)S(1)}, f32[128,512]{1,0:T(8,128)S(1)}, u32[]{:S(2)}, u32[]{:S(2)}) collective-permute-start(f32[128,512]{1,0:T(8,128)S(1)} %slice.151), channel_id=1, source_target_pairs={{0,4},{4,8},{8,12},{12,16},{16,20},{20,24},{24,28},{28,32},{32,36}... | collective-permute-start | bytes 786440 | tf_op jit(solution)/shard_map/ppermute | solution.py:18
  109.4 3.3 %collective-permute-done.1 = f32[128,512]{1,0:T(8,128)S(1)} collective-permute-done((f32[128,512]{1,0:T(8,128)S(1)}, f32[128,512]{1,0:T(8,128)S(1)}, u32[]{:S(2)}, u32[]{:S(2)}) %collective-permute-start.1) | collective-permute-done | bytes 262176 | tf_op jit(solution)/shard_map/ppermute | solution.py:18
  113.6 4.1 %fusion.323 = f32[128,512]{1,0:T(8,128)S(1)} fusion(bf16[128,4096]{0,1:T(8,128)(2,1)} %all-gather.3.cloned.1.call-done, bf16[512,4096]{1,0:T(8,128)(2,1)} %param.14), kind=kOutput, calls=%fused_computation.363 | convolution fusion | flops 536870912 | bytes 5505024 | tf_op jit(solution)/shard_map/dot_general | solution.py:222
  120.5 5.1 %collective-permute-done.2 = bf16[128,512]{1,0:T(8,128)(2,1)S(1)} collective-permute-done((bf16[128,512]{1,0:T(8,128)(2,1)S(1)}, bf16[128,512]{1,0:T(8,128)(2,1)S(1)}, u32[]{:S(2)}, u32[]{:S(2)}) %collective-permute-start.2) | collective-permute-done | bytes 131104 | tf_op jit(solution)/shard_map/ppermute | solution.py:18
  129.4 3.8 %reduce.3 = bf16[128,1024]{1,0:T(8,128)(2,1)} reduce(bf16[128,1,1024]{2,1,0:T(2,128)(2,1)} %bitcast.185, bf16[]{:T(256)} %broadcast.226), dimensions={1}, to_apply=%bitcast.182.reduce_sub_computation | reduce | bytes 524290
  135.0 9.8 %all-to-all-start.3 = ((bf16[64,2,1024]{2,1,0:T(2,128)(2,1)}), bf16[64,2,1024]{2,1,0:T(2,128)(2,1)}, u32[]{:S(2)}, u32[]{:S(2)}) async-start(bf16[64,2,1024]{2,1,0:T(2,128)(2,1)} %reshape.88), calls=%async_computation.4 | async-start | bytes 524288 | tf_op jit(solution)/shard_map/all_to_all | solution.py:248
  145.0 4.4 %fusion.322 = f32[128,4096]{1,0:T(8,128)} fusion(bf16[128,512]{1,0:T(8,128)(2,1)} %get-tuple-element.17, bf16[512,4096]{1,0:T(8,128)(2,1)} %param.14), kind=kOutput, calls=%fused_computation.362 | convolution fusion | flops 536870912 | bytes 6422528 | tf_op jit(solution)/shard_map/dot_general | solution.py:218
  149.4 9.0 %all-to-all-done.3 = bf16[64,2,1024]{2,1,0:T(2,128)(2,1)} async-done(((bf16[64,2,1024]{2,1,0:T(2,128)(2,1)}), bf16[64,2,1024]{2,1,0:T(2,128)(2,1)}, u32[]{:S(2)}, u32[]{:S(2)}) %all-to-all-start.3) | async-done | bytes 262176 | tf_op jit(solution)/shard_map/all_to_all | solution.py:248
  158.4 2.8 reshape.89
  161.2 3.2 %bitcast_reduce_fusion = bf16[128,1024]{1,0:T(8,128)(2,1)} fusion(bf16[128,1,1024]{2,1,0:T(2,128)(2,1)} %reshape.89), kind=kLoop, calls=%fused_computation.360 | loop fusion | bytes 524288 | tf_op jit(solution)/shard_map/all_to_all | solution.py:248
  175.8 22.9 %all_to_all.64 = bf16[64,2,2048]{2,1,0:T(2,128)(2,1)S(1)} all-to-all(bf16[64,2,2048]{2,1,0:T(2,128)(2,1)S(1)} %copy.49), channel_id=1, replica_groups=mesh['seq_hi'=8,'seq_lo'=8,'ch'=4] {'seq_hi','seq_lo'}, dimensions={0} | all-to-all | bytes 1048576 | tf_op jit(solution)/shard_map/all_to_all | solution.py:261
  198.7 3.8 %all-to-all-start.2 = ((bf16[128,8,8,64]{0,3,2,1:T(8,128)(2,1)}), bf16[128,8,8,64]{0,3,2,1:T(8,128)(2,1)S(1)}, u32[]{:S(2)}, u32[]{:S(2)}) async-start(bf16[128,8,8,64]{0,3,2,1:T(8,128)(2,1)} %bitcast.184), calls=%async_computation.2 | async-start | bytes 2097152 | tf_op jit(solution)/shard_map/all_to_all | solution.py:229
  205.6 26.1 %all-to-all-done.2 = bf16[128,8,8,64]{0,3,2,1:T(8,128)(2,1)S(1)} async-done(((bf16[128,8,8,64]{0,3,2,1:T(8,128)(2,1)}), bf16[128,8,8,64]{0,3,2,1:T(8,128)(2,1)S(1)}, u32[]{:S(2)}, u32[]{:S(2)}) %all-to-all-start.2) | async-done | bytes 1048608 | tf_op jit(solution)/shard_map/all_to_all | solution.py:229
  233.4 2.2 fusion.17
  241.8 2.4 collective-permute-start.3
  248.3 12.4 %shard_map.143 = f32[16,512]{1,0:T(8,128)} custom-call(f32[8,16,512]{2,1,0:T(8,128)} %broadcast_in_dim.21.blocks_ref), custom_call_target="tpu_custom_call" | custom-call | tf_op jit(solution)/shard_map/pallas_call | solution.py:82
  262.7 20.9 %shard_map.144 = f32[80,512]{1,0:T(8,128)} custom-call(f32[8,80,512]{2,1,0:T(8,128)} %pad_maximum_fusion.blocks_ref), custom_call_target="tpu_custom_call" | custom-call | tf_op jit(solution)/shard_map/pallas_call | solution.py:82
  (112 shorter events, 66.3 us)
Async XLA Ops:
  7.2 5.4 %copy-start = (f32[128,512]{1,0:T(8,128)S(1)}, f32[128,512]{1,0:T(8,128)}, u32[]{:S(2)}) copy-start(f32[128,512]{1,0:T(8,128)} %param.12) | copy-start | bytes 786436
  8.0 6.9 %collective-permute-start = (bf16[3,2,512]{2,1,0:T(2,128)(2,1)S(1)}, bf16[3,2,512]{2,1,0:T(2,128)(2,1)S(1)}, u32[]{:S(2)}, u32[]{:S(2)}) collective-permute-start(bf16[3,2,512]{2,1,0:T(2,128)(2,1)S(1)} %pad_maximum_fusion.10), channel_id=1, source_target_pairs={{0,4},{4,8},{8,12},{12,16},{16,20},{20,24},{24,28},{28,32},{32,36}... | collective-permute-start | bytes 18440 | tf_op jit(solution)/shard_map/ppermute | solution.py:18
  73.6 39.0 %copy-start.6 = (f32[512]{0:T(512)S(1)}, f32[512]{0:T(512)}, u32[]{:S(2)}) copy-start(f32[512]{0:T(512)} %param.13) | copy-start | bytes 6148
  75.4 24.3 %all-to-all-start.1 = ((f32[64,2,1024]{2,1,0:T(2,128)}), f32[64,2,1024]{2,1,0:T(2,128)}, u32[]{:S(2)}, u32[]{:S(2)}) async-start(f32[64,2,1024]{2,1,0:T(2,128)} %copy.44), calls=%async_computation.1 | async-start | bytes 1048576 | tf_op jit(solution)/shard_map/all_to_all | solution.py:206
  82.1 31.4 %all-gather.3.cloned.1.call-start = ((), (), s32[]{:S(2)}) async-start(), calls=%async_computation.6 | async-start | bytes 1310720 | tf_op jit(solution)/shard_map/all_gather | solution.py:216
  84.0 149.4 %all-gather.5.cloned.1.call-start = ((), (), s32[]{:S(2)}) async-start(), calls=%async_computation.7 | async-start | bytes 1179648 | tf_op jit(solution)/shard_map/all_gather | solution.py:228
  106.0 6.7 %collective-permute-start.1 = (f32[128,512]{1,0:T(8,128)S(1)}, f32[128,512]{1,0:T(8,128)S(1)}, u32[]{:S(2)}, u32[]{:S(2)}) collective-permute-start(f32[128,512]{1,0:T(8,128)S(1)} %slice.151), channel_id=1, source_target_pairs={{0,4},{4,8},{8,12},{12,16},{16,20},{20,24},{24,28},{28,32},{32,36}... | collective-permute-start | bytes 786440 | tf_op jit(solution)/shard_map/ppermute | solution.py:18
  113.6 4.1 %copy-start.4 = (f32[128,512]{1,0:T(8,128)S(1)}, f32[128,512]{1,0:T(8,128)}, u32[]{:S(2)}) copy-start(f32[128,512]{1,0:T(8,128)} %get-tuple-element.30) | copy-start | bytes 786436
  118.5 8.1 %copy-start.2 = (f32[128,512]{1,0:T(8,128)}, f32[128,512]{1,0:T(8,128)S(1)}, u32[]{:S(2)}) copy-start(f32[128,512]{1,0:T(8,128)S(1)} %get-tuple-element.28) | copy-start | bytes 786436
  118.5 7.0 %collective-permute-start.2 = (bf16[128,512]{1,0:T(8,128)(2,1)S(1)}, bf16[128,512]{1,0:T(8,128)(2,1)S(1)}, u32[]{:S(2)}, u32[]{:S(2)}) collective-permute-start(bf16[128,512]{1,0:T(8,128)(2,1)S(1)} %convert_element_type.112), channel_id=1, source_target_pairs={{4,0},{8,4},{12,8},{16,12},{20,16},{24,20},{28,24},{32,28},{36,32}... | collective-permute-start | bytes 393224 | tf_op jit(solution)/shard_map/ppermute | solution.py:18
  135.0 23.4 %all-to-all-start.3 = ((bf16[64,2,1024]{2,1,0:T(2,128)(2,1)}), bf16[64,2,1024]{2,1,0:T(2,128)(2,1)}, u32[]{:S(2)}, u32[]{:S(2)}) async-start(bf16[64,2,1024]{2,1,0:T(2,128)(2,1)} %reshape.88), calls=%async_computation.4 | async-start | bytes 524288 | tf_op jit(solution)/shard_map/all_to_all | solution.py:248
  144.8 90.9 %reduce-scatter.2.cloned.1.call-start = ((), (), s32[]{:S(2)}) async-start(), calls=%async_computation.8 | async-start | bytes 2621440 | tf_op jit(solution)/shard_map/reduce_scatter | solution.py:219
  198.7 32.9 %all-to-all-start.2 = ((bf16[128,8,8,64]{0,3,2,1:T(8,128)(2,1)}), bf16[128,8,8,64]{0,3,2,1:T(8,128)(2,1)S(1)}, u32[]{:S(2)}, u32[]{:S(2)}) async-start(bf16[128,8,8,64]{0,3,2,1:T(8,128)(2,1)} %bitcast.184), calls=%async_computation.2 | async-start | bytes 2097152 | tf_op jit(solution)/shard_map/all_to_all | solution.py:229
  203.6 36.6 %copy-start.3 = (f32[128,512]{1,0:T(8,128)S(1)}, f32[128,512]{1,0:T(8,128)}, u32[]{:S(2)}) copy-start(f32[128,512]{1,0:T(8,128)} %copy-done.2) | copy-start | bytes 786436
  231.7 10.0 %copy-start.1 = (f32[1,128,512]{2,1,0:T(8,128)S(1)}, f32[1,128,512]{2,1,0:T(8,128)}, u32[]{:S(2)}) copy-start(f32[1,128,512]{2,1,0:T(8,128)} %get-tuple-element.53) | copy-start | bytes 786436
  235.7 8.6 %copy-start.5 = (bf16[1,128,512]{2,1,0:T(8,128)(2,1)S(1)}, bf16[1,128,512]{2,1,0:T(8,128)(2,1)}, u32[]{:S(2)}) copy-start(bf16[1,128,512]{2,1,0:T(8,128)(2,1)} %get-tuple-element.23) | copy-start | bytes 393220
  241.8 5.0 %collective-permute-start.3 = (f32[3,2,512]{2,1,0:T(2,128)S(1)}, f32[3,2,512]{2,1,0:T(2,128)S(1)}, u32[]{:S(2)}, u32[]{:S(2)}) collective-permute-start(f32[3,2,512]{2,1,0:T(2,128)S(1)} %slice.158), channel_id=1, source_target_pairs={{4,0},{8,4},{12,8},{16,12},{20,16},{24,20},{28,24},{32,28},{36,32}... | collective-permute-start | bytes 36872 | tf_op jit(solution)/shard_map/ppermute | solution.py:18
Sparse Core Ops, SparseCore 0:
  85.3 26.5 all-gather.2
  114.3 36.7 all-gather.4
  153.6 35.5 reduce-scatter.1
where the time goes:
time: 301 us; the launch traced here: 296 us
  blocking collectives  63.1 us (21%)
  waiting for transfers between devices  60.7 us (20%)
  matrix products  41.9 us (14%)
  local copies, waits for them, and re-layouts  33.7 us (11%)
  Pallas kernels  33.3 us (11%)
  starting transfers between devices  32.9 us (11%)
  other arithmetic  15.4 us (5%)
  between operations  14.7 us (5%)
    all_to_all x1, blocking collectives, on_device(): lax.all_to_all(jnp.concatenate([input_pair[0], input_pair[1], filter_pair...  40.2 us
    pallas_call x2, Pallas kernels, sum_over_group(): pl.pallas_call(functools.partial(group_sum_kernel, axis), out_shape=jax.S...  33.3 us
    dot_general x36, matrix products, along_rows(): return jnp.tensordot(factor, values, axes=1, precision=exact_mode)  31.2 us
    all_to_all x1, waiting for transfers between devices, on_device(): lax.all_to_all(full_cotangent.reshape(block_rows, outer, inner, feature_r...  26.1 us
    all_to_all x1, blocking collectives, on_device(): lax.all_to_all(as_sent(jnp.concatenate(input_back + filter_back, axis=-1)...  22.9 us
    all_to_all x1, waiting for transfers between devices, on_device(): lax.all_to_all(jnp.concatenate(inverse_pair, axis=-1), SEQ, split_axis=0,...  15.7 us
    ppermute x4, starting transfers between devices, from_behind(): return lax.ppermute(shard, axis, pairs)  12.3 us
    ppermute x4, waiting for transfers between devices, from_behind(): return lax.ppermute(shard, axis, pairs)  9.8 us
  transfers between devices with their start and end apart: 10, of which 6 were waited for; matrix products, arithmetic and copies ran while one was open for 17% of the time, Pallas kernels for 0%

commit v1 on v0

--- a/solution.py
+++ b/solution.py
@@ -267,8 +267,9 @@
         ),
         lanes,
     )
-    weight_terms, layer_out, returned_grad = lax.optimization_barrier(
-        (weight_terms, layer_out, returned_grad)
+    grad_w_out_t = lax.psum_scatter(weight_terms, "seq_lo", scatter_dimension=0, tiled=True)
+    grad_w_out_t, layer_out, returned_grad = lax.optimization_barrier(
+        (grad_w_out_t, layer_out, returned_grad)
     )
     conv_grad = rows_inverse((returned_grad[0][0], returned_grad[1][0]), half_basis)
     grad_filter = rows_inverse((returned_grad[2][0], returned_grad[3][0]), half_basis)
@@ -301,17 +302,9 @@
     outer_sum = sum_over_group(
         jnp.broadcast_to(small_terms, (outer,) + small_terms.shape), "seq_hi", 0
     )
-    weight_blocks = weight_terms.reshape(inner, -1, channel_count)
-    block_height = weight_blocks.shape[1]
-    reduced = sum_over_group(
-        jnp.concatenate(
-            [weight_blocks, jnp.broadcast_to(outer_sum, (inner,) + outer_sum.shape)], axis=1
-        ),
-        "seq_lo",
-        1,
-    )
-    grad_w_out_t = reduced[:block_height]
-    summed = reduced[block_height:]
+    summed = sum_over_group(
+        jnp.broadcast_to(outer_sum, (inner,) + outer_sum.shape), "seq_lo", 1
+    )
     grad_short = summed[: sum_rows - 1].reshape(short_terms.shape)
     grad_skip = summed[sum_rows - 1]
     return (

time: 301 us -> 282 us (0.937)
  Pallas kernels: 33.3 us -> 23.8 us
  waiting for transfers between devices: 60.7 us -> 54 us
    all_to_all x1, waiting for transfers between devices: 26.1 us -> 11.8 us  [on_device(): lax.all_to_all(full_cotangent.reshape(block_rows, outer, inner, feature_r...]
    pallas_call x2, Pallas kernels: 33.3 us -> 23.8 us  [sum_over_group(): pl.pallas_call(functools.partial(group_sum_kernel, axis), out_shape=jax.S...]
    all_to_all x1, waiting for transfers between devices: 8.99 us -> 17.6 us  [on_device(): lax.all_to_all(as_sent(jnp.concatenate(input_back + filter_back, axis=-1)...]
    all_to_all x1, starting transfers between devices: 9.79 us -> 4.92 us  [on_device(): lax.all_to_all(as_sent(jnp.concatenate(input_back + filter_back, axis=-1)...]
    unnamed x20 -> x26, local copies, waits for them, and re-layouts: 6.87 us -> 6.89 us
  transfers between devices with their start and end apart: 10 -> 11, of which waited for: 6 -> 5; matrix products, arithmetic and copies ran while one was open for 17% -> 20% of each run, Pallas kernels for 0% -> 0%
where the time goes in v1:
time: 282 us; the launch traced here: 276 us
  blocking collectives  63.9 us (23%)
  waiting for transfers between devices  54 us (19%)
  matrix products  40.7 us (14%)
  local copies, waits for them, and re-layouts  32.3 us (11%)
  starting transfers between devices  30.9 us (11%)
  Pallas kernels  23.8 us (8%)
  other arithmetic  16.1 us (6%)
  between operations  14.7 us (5%)
    all_to_all x1, blocking collectives, on_device(): lax.all_to_all(jnp.concatenate([input_pair[0], input_pair[1], filter_pair...  40.2 us
    dot_general x36, matrix products, along_rows(): return jnp.tensordot(factor, values, axes=1, precision=exact_mode)  30.6 us
    pallas_call x2, Pallas kernels, sum_over_group(): pl.pallas_call(functools.partial(group_sum_kernel, axis), out_shape=jax.S...  23.8 us
    all_to_all x1, blocking collectives, on_device(): lax.all_to_all(jnp.concatenate(grad_pair, axis=1)[None].astype(jnp.bfloat...  23.7 us
    all_to_all x1, waiting for transfers between devices, on_device(): lax.all_to_all(as_sent(jnp.concatenate(input_back + filter_back, axis=-1)...  17.6 us
    all_to_all x1, waiting for transfers between devices, on_device(): lax.all_to_all(jnp.concatenate(inverse_pair, axis=-1), SEQ, split_axis=0,...  15.7 us
    ppermute x4, starting transfers between devices, from_behind(): return lax.ppermute(shard, axis, pairs)  14.7 us
    all_to_all x1, waiting for transfers between devices, on_device(): lax.all_to_all(full_cotangent.reshape(block_rows, outer, inner, feature_r...  11.8 us
  transfers between devices with their start and end apart: 11, of which 5 were waited for; matrix products, arithmetic and copies ran while one was open for 20% of the time, Pallas kernels for 0%

profile of v1, /device:TPU:1, one launch (start us, length us, event | category | flops | bytes accessed | tf_op | source)
XLA Modules:
  0.0 276.4 jit_solution(9961403587061397351)
XLA Ops:
  8.0 4.6 %collective-permute-start = (bf16[3,2,512]{2,1,0:T(2,128)(2,1)S(1)}, bf16[3,2,512]{2,1,0:T(2,128)(2,1)S(1)}, u32[]{:S(2)}, u32[]{:S(2)}) collective-permute-start(bf16[3,2,512]{2,1,0:T(2,128)(2,1)S(1)} %pad_maximum_fusion.9), channel_id=1, source_target_pairs={{0,4},{4,8},{8,12},{12,16},{16,20},{20,24},{24,28},{28,32},{32,36}... | collective-permute-start | bytes 18440 | tf_op jit(solution)/shard_map/ppermute | solution.py:18
  18.9 40.2 %all_to_all.63 = f32[1,128,2048]{2,0,1:T(1,128)S(1)} all-to-all(f32[1,128,2048]{2,0,1:T(1,128)S(1)} %copy.39), channel_id=1, replica_groups=mesh['seq_hi'=8,'seq_lo'=8,'ch'=4] {'seq_hi','seq_lo'}, dimensions={1} | all-to-all | bytes 2097152 | tf_op jit(solution)/shard_map/all_to_all | solution.py:191
  59.0 3.7 %reduce = f32[128,2048]{1,0:T(8,128)} reduce(f32[1,128,2048]{2,0,1:T(1,128)S(1)} %all_to_all.63, f32[]{:T(128)} %constant.83), dimensions={0}, to_apply=%all_to_all.22.reduce_sub_computation | reduce | bytes 2097156 | tf_op jit(solution)/shard_map/all_to_all | solution.py:191
  75.5 6.7 %all-to-all-start.1 = ((f32[64,2,1024]{2,1,0:T(2,128)}), f32[64,2,1024]{2,1,0:T(2,128)}, u32[]{:S(2)}, u32[]{:S(2)}) async-start(f32[64,2,1024]{2,1,0:T(2,128)} %copy.44), calls=%async_computation.1 | async-start | bytes 1048576 | tf_op jit(solution)/shard_map/all_to_all | solution.py:206
  84.1 15.7 %all-to-all-done.1 = f32[64,2,1024]{2,1,0:T(2,128)} async-done(((f32[64,2,1024]{2,1,0:T(2,128)}), f32[64,2,1024]{2,1,0:T(2,128)}, u32[]{:S(2)}, u32[]{:S(2)}) %all-to-all-start.1) | async-done | bytes 524320 | tf_op jit(solution)/shard_map/all_to_all | solution.py:206
  99.8 2.2 all_to_all.50
  106.0 3.4 %collective-permute-start.1 = (f32[128,512]{1,0:T(8,128)S(1)}, f32[128,512]{1,0:T(8,128)S(1)}, u32[]{:S(2)}, u32[]{:S(2)}) collective-permute-start(f32[128,512]{1,0:T(8,128)S(1)} %slice.144), channel_id=1, source_target_pairs={{0,4},{4,8},{8,12},{12,16},{16,20},{20,24},{24,28},{28,32},{32,36}... | collective-permute-start | bytes 786440 | tf_op jit(solution)/shard_map/ppermute | solution.py:18
  109.4 3.3 %collective-permute-done.1 = f32[128,512]{1,0:T(8,128)S(1)} collective-permute-done((f32[128,512]{1,0:T(8,128)S(1)}, f32[128,512]{1,0:T(8,128)S(1)}, u32[]{:S(2)}, u32[]{:S(2)}) %collective-permute-start.1) | collective-permute-done | bytes 262176 | tf_op jit(solution)/shard_map/ppermute | solution.py:18
  113.7 4.9 %fusion.323 = f32[128,512]{1,0:T(8,128)} fusion(bf16[128,4096]{0,1:T(8,128)(2,1)} %all-gather.3.cloned.1.call-done, bf16[512,4096]{1,0:T(8,128)(2,1)} %param.14), kind=kOutput, calls=%fused_computation.362 | convolution fusion | flops 536870912 | bytes 5505024 | tf_op jit(solution)/shard_map/dot_general | solution.py:222
  124.4 5.5 %collective-permute-done.2 = bf16[128,512]{1,0:T(8,128)(2,1)S(1)} collective-permute-done((bf16[128,512]{1,0:T(8,128)(2,1)S(1)}, bf16[128,512]{1,0:T(8,128)(2,1)S(1)}, u32[]{:S(2)}, u32[]{:S(2)}) %collective-permute-start.2) | collective-permute-done | bytes 131104 | tf_op jit(solution)/shard_map/ppermute | solution.py:18
  133.8 3.8 %reduce.3 = bf16[128,1024]{1,0:T(8,128)(2,1)} reduce(bf16[128,1,1024]{2,1,0:T(2,128)(2,1)} %bitcast.184, bf16[]{:T(256)} %broadcast.226), dimensions={1}, to_apply=%bitcast.181.reduce_sub_computation | reduce | bytes 524290
  139.4 23.7 %all_to_all.64 = bf16[64,2,1024]{2,1,0:T(2,128)(2,1)} all-to-all(bf16[64,2,1024]{2,1,0:T(2,128)(2,1)} %reshape.84), channel_id=1, replica_groups=mesh['seq_hi'=8,'seq_lo'=8,'ch'=4] {'seq_hi','seq_lo'}, dimensions={0} | all-to-all | bytes 524288 | tf_op jit(solution)/shard_map/all_to_all | solution.py:248
  163.1 4.2 %all-to-all-start.2 = ((bf16[128,8,8,64]{0,3,2,1:T(8,128)(2,1)}), bf16[128,8,8,64]{0,3,2,1:T(8,128)(2,1)}, u32[]{:S(2)}, u32[]{:S(2)}) async-start(bf16[128,8,8,64]{0,3,2,1:T(8,128)(2,1)} %bitcast.183), calls=%async_computation.2 | async-start | bytes 2097152 | tf_op jit(solution)/shard_map/all_to_all | solution.py:229
  167.6 2.8 %reshape.85 = bf16[128,1,1024]{2,1,0:T(2,128)(2,1)} reshape(bf16[64,2,1024]{2,1,0:T(2,128)(2,1)} %all_to_all.64) | data formatting | bytes 524288
  170.4 3.2 %bitcast_reduce_fusion = bf16[128,1024]{1,0:T(8,128)(2,1)} fusion(bf16[128,1,1024]{2,1,0:T(2,128)(2,1)} %reshape.85), kind=kLoop, calls=%fused_computation.359 | loop fusion | bytes 524288 | tf_op jit(solution)/shard_map/all_to_all | solution.py:248
  178.2 2.6 multiply_add_fusion.2
  184.9 11.8 %all-to-all-done.2 = bf16[128,8,8,64]{0,3,2,1:T(8,128)(2,1)} async-done(((bf16[128,8,8,64]{0,3,2,1:T(8,128)(2,1)}), bf16[128,8,8,64]{0,3,2,1:T(8,128)(2,1)}, u32[]{:S(2)}, u32[]{:S(2)}) %all-to-all-start.2) | async-done | bytes 1048608 | tf_op jit(solution)/shard_map/all_to_all | solution.py:229
  196.6 2.9 %copy.45 = bf16[8,128,1,8,64]{1,0,4,3,2:T(8,128)(2,1)} copy(bf16[8,128,1,8,64]{1,4,3,0,2:T(8,128)(2,1)} %bitcast.15) | data formatting | bytes 2097152 | tf_op jit(solution)/shard_map/all_to_all | solution.py:229
  199.6 3.2 %fusion.17 = f32[512,512]{1,0:T(8,128)} fusion(bf16[1024,512]{1,0:T(8,128)(2,1)} %all-gather.5.cloned.1.call-done, bf16[64,8,8,128]{3,2,1,0:T(8,128)(2,1)} %bitcast.185), kind=kOutput, calls=%fused_computation.36 | convolution fusion | flops 536870912 | bytes 3145728 | tf_op jit(solution)/shard_map/dot_general | solution.py:236
  206.9 4.9 %all-to-all-start.4 = ((bf16[64,2,2048]{2,1,0:T(2,128)(2,1)}), bf16[64,2,2048]{2,1,0:T(2,128)(2,1)S(1)}, u32[]{:S(2)}, u32[]{:S(2)}) async-start(bf16[64,2,2048]{2,1,0:T(2,128)(2,1)} %copy.49), calls=%async_computation.6 | async-start | bytes 1048576 | tf_op jit(solution)/shard_map/all_to_all | solution.py:261
  211.9 17.6 %all-to-all-done.4 = bf16[64,2,2048]{2,1,0:T(2,128)(2,1)S(1)} async-done(((bf16[64,2,2048]{2,1,0:T(2,128)(2,1)}), bf16[64,2,2048]{2,1,0:T(2,128)(2,1)S(1)}, u32[]{:S(2)}, u32[]{:S(2)}) %all-to-all-start.4) | async-done | bytes 524320 | tf_op jit(solution)/shard_map/all_to_all | solution.py:261
  233.2 4.8 %collective-permute-start.3 = (f32[3,2,512]{2,1,0:T(2,128)S(1)}, f32[3,2,512]{2,1,0:T(2,128)S(1)}, u32[]{:S(2)}, u32[]{:S(2)}) collective-permute-start(f32[3,2,512]{2,1,0:T(2,128)S(1)} %slice.151), channel_id=1, source_target_pairs={{4,0},{8,4},{12,8},{16,12},{20,16},{24,20},{28,24},{32,28},{36,32}... | collective-permute-start | bytes 36872 | tf_op jit(solution)/shard_map/ppermute | solution.py:18
  240.7 14.5 %shard_map.143 = f32[16,512]{1,0:T(8,128)} custom-call(f32[8,16,512]{2,1,0:T(8,128)} %broadcast_in_dim.21.blocks_ref), custom_call_target="tpu_custom_call" | custom-call | tf_op jit(solution)/shard_map/pallas_call | solution.py:82
  256.7 9.4 %shard_map.144 = f32[16,512]{1,0:T(8,128)} custom-call(f32[8,16,512]{2,1,0:T(8,128)} %broadcast_in_dim.22.blocks_ref), custom_call_target="tpu_custom_call" | custom-call | tf_op jit(solution)/shard_map/pallas_call | solution.py:82
  (118 shorter events, 62.1 us)
Async XLA Ops:
  7.2 5.4 %copy-start = (f32[128,512]{1,0:T(8,128)S(1)}, f32[128,512]{1,0:T(8,128)}, u32[]{:S(2)}) copy-start(f32[128,512]{1,0:T(8,128)} %param.12) | copy-start | bytes 786436
  8.0 6.9 %collective-permute-start = (bf16[3,2,512]{2,1,0:T(2,128)(2,1)S(1)}, bf16[3,2,512]{2,1,0:T(2,128)(2,1)S(1)}, u32[]{:S(2)}, u32[]{:S(2)}) collective-permute-start(bf16[3,2,512]{2,1,0:T(2,128)(2,1)S(1)} %pad_maximum_fusion.9), channel_id=1, source_target_pairs={{0,4},{4,8},{8,12},{12,16},{16,20},{20,24},{24,28},{28,32},{32,36}... | collective-permute-start | bytes 18440 | tf_op jit(solution)/shard_map/ppermute | solution.py:18
  73.7 39.1 %copy-start.9 = (f32[512]{0:T(512)S(1)}, f32[512]{0:T(512)}, u32[]{:S(2)}) copy-start(f32[512]{0:T(512)} %param.13) | copy-start | bytes 6148
  75.5 24.3 %all-to-all-start.1 = ((f32[64,2,1024]{2,1,0:T(2,128)}), f32[64,2,1024]{2,1,0:T(2,128)}, u32[]{:S(2)}, u32[]{:S(2)}) async-start(f32[64,2,1024]{2,1,0:T(2,128)} %copy.44), calls=%async_computation.1 | async-start | bytes 1048576 | tf_op jit(solution)/shard_map/all_to_all | solution.py:206
  82.2 31.4 %all-gather.3.cloned.1.call-start = ((), (), s32[]{:S(2)}) async-start(), calls=%async_computation.7 | async-start | bytes 1310720 | tf_op jit(solution)/shard_map/all_gather | solution.py:216
  84.0 115.5 %all-gather.5.cloned.1.call-start = ((), (), s32[]{:S(2)}) async-start(), calls=%async_computation.8 | async-start | bytes 1179648 | tf_op jit(solution)/shard_map/all_gather | solution.py:228
  106.0 6.7 %collective-permute-start.1 = (f32[128,512]{1,0:T(8,128)S(1)}, f32[128,512]{1,0:T(8,128)S(1)}, u32[]{:S(2)}, u32[]{:S(2)}) collective-permute-start(f32[128,512]{1,0:T(8,128)S(1)} %slice.144), channel_id=1, source_target_pairs={{0,4},{4,8},{8,12},{12,16},{16,20},{20,24},{24,28},{28,32},{32,36}... | collective-permute-start | bytes 786440 | tf_op jit(solution)/shard_map/ppermute | solution.py:18
  113.6 116.2 %reduce-scatter.5.cloned.1.call-start = ((), (), s32[]{:S(2)}) async-start(), calls=%async_computation.10 | async-start | bytes 2621440 | tf_op jit(solution)/shard_map/reduce_scatter | solution.py:219
  113.7 4.9 %copy-start.1 = (bf16[512,4096]{1,0:T(8,128)(2,1)S(1)}, bf16[512,4096]{1,0:T(8,128)(2,1)}, u32[]{:S(2)}) copy-start(bf16[512,4096]{1,0:T(8,128)(2,1)} %param.14) | copy-start | bytes 12582916
  113.7 4.9 %copy-start.8 = (bf16[128,512]{1,0:T(8,128)(2,1)S(1)}, bf16[128,512]{1,0:T(8,128)(2,1)}, u32[]{:S(2)}) copy-start(bf16[128,512]{1,0:T(8,128)(2,1)} %get-tuple-element.17) | copy-start | bytes 393220
  122.5 8.5 %copy-start.6 = (f32[128,512]{1,0:T(8,128)}, f32[128,512]{1,0:T(8,128)S(1)}, u32[]{:S(2)}) copy-start(f32[128,512]{1,0:T(8,128)S(1)} %get-tuple-element.28) | copy-start | bytes 786436
  122.5 7.4 %collective-permute-start.2 = (bf16[128,512]{1,0:T(8,128)(2,1)S(1)}, bf16[128,512]{1,0:T(8,128)(2,1)S(1)}, u32[]{:S(2)}, u32[]{:S(2)}) collective-permute-start(bf16[128,512]{1,0:T(8,128)(2,1)S(1)} %convert_element_type.112), channel_id=1, source_target_pairs={{4,0},{8,4},{12,8},{16,12},{20,16},{24,20},{28,24},{32,28},{36,32}... | collective-permute-start | bytes 393224 | tf_op jit(solution)/shard_map/ppermute | solution.py:18
  163.1 33.5 %all-to-all-start.2 = ((bf16[128,8,8,64]{0,3,2,1:T(8,128)(2,1)}), bf16[128,8,8,64]{0,3,2,1:T(8,128)(2,1)}, u32[]{:S(2)}, u32[]{:S(2)}) async-start(bf16[128,8,8,64]{0,3,2,1:T(8,128)(2,1)} %bitcast.183), calls=%async_computation.2 | async-start | bytes 2097152 | tf_op jit(solution)/shard_map/all_to_all | solution.py:229
  167.4 64.2 %reduce-scatter.3.cloned.1.call-start = ((), (), s32[]{:S(2)}) async-start(), calls=%async_computation.9 | async-start | bytes 1179648 | tf_op jit(solution)/shard_map/reduce_scatter | solution.py:270
  180.9 2.8 %copy-start.3 = (f32[128,2,512]{2,0,1:T(8,128)}, f32[128,2,512]{2,0,1:T(8,128)S(1)}, u32[]{:S(2)}) copy-start(f32[128,2,512]{2,0,1:T(8,128)S(1)} %get-tuple-element.40) | copy-start | bytes 1572868
  182.5 20.3 %copy-start.2 = (f32[128,2,512]{2,0,1:T(8,128)S(1)}, f32[128,2,512]{2,0,1:T(8,128)}, u32[]{:S(2)}) copy-start(f32[128,2,512]{2,0,1:T(8,128)} %get-tuple-element.39) | copy-start | bytes 1572868
  184.9 19.1 %copy-start.4 = (f32[128,2,512]{2,0,1:T(8,128)S(1)}, f32[128,2,512]{2,0,1:T(8,128)}, u32[]{:S(2)}) copy-start(f32[128,2,512]{2,0,1:T(8,128)} %copy-done.3) | copy-start | bytes 1572868
  203.4 29.2 %copy-start.7 = (f32[128,512]{1,0:T(8,128)S(1)}, f32[128,512]{1,0:T(8,128)}, u32[]{:S(2)}) copy-start(f32[128,512]{1,0:T(8,128)} %copy-done.6) | copy-start | bytes 786436
  204.5 28.6 %copy-start.5 = (f32[1,128,512]{2,1,0:T(8,128)S(1)}, f32[1,128,512]{2,1,0:T(8,128)}, u32[]{:S(2)}) copy-start(f32[1,128,512]{2,1,0:T(8,128)} %get-tuple-element.53) | copy-start | bytes 786436
  206.9 22.6 %all-to-all-start.4 = ((bf16[64,2,2048]{2,1,0:T(2,128)(2,1)}), bf16[64,2,2048]{2,1,0:T(2,128)(2,1)S(1)}, u32[]{:S(2)}, u32[]{:S(2)}) async-start(bf16[64,2,2048]{2,1,0:T(2,128)(2,1)} %copy.49), calls=%async_computation.6 | async-start | bytes 1048576 | tf_op jit(solution)/shard_map/all_to_all | solution.py:261
  233.2 6.0 %collective-permute-start.3 = (f32[3,2,512]{2,1,0:T(2,128)S(1)}, f32[3,2,512]{2,1,0:T(2,128)S(1)}, u32[]{:S(2)}, u32[]{:S(2)}) collective-permute-start(f32[3,2,512]{2,1,0:T(2,128)S(1)} %slice.151), channel_id=1, source_target_pairs={{4,0},{8,4},{12,8},{16,12},{20,16},{24,20},{28,24},{32,28},{36,32}... | collective-permute-start | bytes 36872 | tf_op jit(solution)/shard_map/ppermute | solution.py:18
Sparse Core Ops, SparseCore 0:
  85.4 26.5 all-gather.2
  114.3 36.1 all-gather.4
  153.1 35.3 reduce-scatter.4
  202.9 28.0 reduce-scatter.2
